TPU v7x, 32 devices: a whole 2x2x4 slice. The times are simulated.
32 devices in a mesh: groups: 2 (over y), ctx: 4 (over z), head: 2 (over x), sess: 2 (over core).
Axes of the slice: x: 2, y: 2, z: 4, core: 2. Of those that a mesh axis runs over, the one named last changes fastest.
Arguments:
- head_input: bfloat16 [8, 512, 8192], P(('groups', 'sess'), 'ctx', 'head'), parts along dimension 0, may hold values from -6 to 6
- gate_input: bfloat16 [8, 512, 8192], P(('groups', 'sess'), 'ctx', 'head'), parts along dimension 0, may hold values from -6 to 6
- state_in_proj: bfloat16 [8, 512, 8, 128], P(('groups', 'sess'), 'ctx'), parts along dimension 0, may hold values from -1.796875 to 1.796875
- state_out_proj: bfloat16 [8, 512, 8, 128], P(('groups', 'sess'), 'ctx'), parts along dimension 0, may hold values from -1.796875 to 1.796875
- step_raw: float32 [8, 512, 128], P(('groups', 'sess'), 'ctx', 'head'), parts along dimension 0, may hold values from -2.5 to 12.5
- head_step_bias: float32 [128], P('head'), may hold values from -5.3 to -2.25
- decay_log: float32 [128], P('head'), may hold values from -7.7 to 0
- skip_gain: float32 [128], P('head'), may hold values from 0.5 to 2
- norm_gain: float32 [8192], P('head'), may hold values from 0.1 to 1.9
- out_weight: bfloat16 [8192, 4096], P('head', 'ctx'), may hold values from -0.09375 to 0.09375
- pool_states: float32 [16, 128, 64, 128], P(('groups', 'sess'), 'head', None, 'ctx'), parts along dimension 0, may hold values from -6 to 6
- slot_map: int32 [8], P('groups'), parts along dimension 0, may hold values from 0 to 7, as said below
- span_lengths: int32 [8], P('groups'), parts along dimension 0, may hold values from 1 to 4, as said below
Outputs:
- mixed: bfloat16 [8, 512, 4096], P(('groups', 'sess'), 'ctx', 'head'), parts along dimension 0
- final_states: float32 [8, 128, 64, 128], P(('groups', 'sess'), 'head', None, 'ctx'), parts along dimension 0
There are 2 independent parts, one for each index of `groups`. A program takes and returns all parts, laid end to end along the dimension named above; an argument that names none is the same for every part. Nothing has to cross between parts.
Inputs may be any that keep to these rules, and one draw needn't show every extreme that they name: `slot_map`: the sessions of a group take distinct decode slots. `span_lengths`: some session of every group fills all 4 units.
All inputs are finite; a program needn't handle non-finite values.
Results may differ from a plain program's by a relative error of at most 0.018.
Values may be sent and summed in bfloat16 or wider, within the bound.
A program may use at most 128 MiB of HBM per device.

v0:
```python
import jax
import jax.numpy as jnp
from jax import lax
from jax.sharding import PartitionSpec as P

HEADS = 128
GROUPS = 8
SPAN = 128
highest = lax.Precision.HIGHEST
norm_eps = 1e-05


def shifted(value, axis, by):
    length = lax.axis_size(axis)
    pairs = [(i, i + by) for i in range(length) if 0 <= i + by < length]
    return lax.ppermute(value, axis, pairs)


def from_root(block, axis, owner):
    block = jnp.where(lax.axis_index(axis) == owner, block, jnp.zeros_like(block))
    return lax.psum(block, axis)


def shards(
    head_input,
    gate_input,
    state_in_proj,
    state_out_proj,
    step_raw,
    head_step_bias,
    decay_log,
    skip_gain,
    norm_gain,
    out_weight,
    pool_states,
    slot_map,
    span_lengths,
):
    ctx_count = lax.axis_size("ctx")
    ctx_index = lax.axis_index("ctx")
    sess_index = lax.axis_index("sess")
    head_index = lax.axis_index("head")
    sessions, tokens, inner = head_input.shape
    heads = step_raw.shape[2]
    head_dim = inner // heads
    state_cols = pool_states.shape[3]
    group_heads = HEADS // GROUPS
    spans = tokens // SPAN
    first_session = sess_index * sessions
    own_lengths = lax.dynamic_slice_in_dim(span_lengths, first_session, sessions)
    position = ctx_index * tokens + jnp.arange(tokens, dtype=jnp.int32)
    live_rows = (position[None, :] < own_lengths[:, None] * SPAN).astype(jnp.float32)
    step_size = jax.nn.softplus(step_raw + head_step_bias) * live_rows[:, :, None]
    log_keep = -jnp.exp(decay_log) * step_size
    pooled = lax.all_gather(pool_states.astype(jnp.bfloat16), "sess", axis=0, tiled=True).astype(
        pool_states.dtype
    )
    own_slots = lax.dynamic_slice_in_dim(slot_map, first_session, sessions)
    start_cols = jnp.take(pooled, own_slots, axis=0)
    start_state = lax.all_gather(start_cols.astype(jnp.bfloat16), "ctx", axis=3, tiled=True).astype(
        start_cols.dtype
    )
    first_head = head_index * heads
    group_count = max(1, heads // group_heads)
    repeats = min(heads, group_heads)
    first_group = first_head // group_heads
    state_size = state_in_proj.shape[3]
    group_shape = (sessions, spans, SPAN, group_count, state_size)
    b_groups = (
        lax.dynamic_slice_in_dim(state_in_proj, first_group, group_count, 2)
        .astype(jnp.float32)
        .reshape(group_shape)
    )
    c_groups = (
        lax.dynamic_slice_in_dim(state_out_proj, first_group, group_count, 2)
        .astype(jnp.float32)
        .reshape(group_shape)
    )
    b_heads = jnp.repeat(b_groups, repeats, axis=3)
    c_heads = jnp.repeat(c_groups, repeats, axis=3)
    inputs = head_input.astype(jnp.float32).reshape(sessions, spans, SPAN, heads, head_dim)
    cum_log = jnp.cumsum(log_keep.reshape(sessions, spans, SPAN, heads), axis=2)
    cum_heads = jnp.moveaxis(cum_log, 3, 2)
    size_heads = jnp.moveaxis(step_size.reshape(sessions, spans, SPAN, heads), 3, 2)
    causal = jnp.arange(SPAN)[:, None] >= jnp.arange(SPAN)[None, :]
    log_gap = cum_heads[..., :, None] - cum_heads[..., None, :]
    decay_pairs = (
        jnp.where(causal, jnp.exp(jnp.where(causal, log_gap, 0.0)), 0.0) * size_heads[..., None, :]
    )
    products_cb = jnp.einsum("sclgn,scmgn->scglm", c_groups, b_groups, precision=highest)
    score_values = jnp.repeat(products_cb, repeats, axis=2) * decay_pairs
    inside_span = jnp.einsum("schlm,scmhp->sclhp", score_values, inputs, precision=highest)
    tail_weight = jnp.exp(cum_heads[..., -1:] - cum_heads) * size_heads
    span_states = jnp.einsum(
        "schm,scmhp,scmhn->schpn", tail_weight, inputs, b_heads, precision=highest
    )
    span_log = cum_heads[..., -1]
    running = jnp.zeros((sessions, heads, head_dim, state_size), jnp.float32)
    entering = [running]
    running = jnp.exp(span_log[:, 0])[..., None, None] * running + span_states[:, 0]
    local_end = running
    shard_log = jnp.sum(span_log, axis=1)
    entry_states = jnp.stack(entering, axis=1)
    prior_log = jnp.cumsum(span_log, axis=1) - span_log
    from_entry = (
        jnp.einsum("sclhn,schpn->sclhp", c_heads, entry_states, precision=highest)
        * jnp.exp(cum_log)[..., None]
    )

    def relay_turn(turn_index, carried):
        outgoing = jnp.exp(shard_log)[..., None, None] * carried + local_end
        incoming = shifted(outgoing.astype(jnp.bfloat16), "ctx", 1).astype(outgoing.dtype)
        return jnp.where(ctx_index == 0, start_state, incoming)

    carried = lax.fori_loop(0, ctx_count - 1, relay_turn, start_state)
    from_start = cum_log + prior_log[:, :, None, :]
    from_carry = (
        jnp.einsum("sclhn,shpn->sclhp", c_heads, carried, precision=highest)
        * jnp.exp(from_start)[..., None]
    )
    ssd_out = inside_span + from_entry + from_carry + skip_gain[:, None] * inputs
    gated = ssd_out.reshape(sessions, tokens, inner) * jax.nn.silu(gate_input.astype(jnp.float32))
    grouped = gated.reshape(sessions, tokens, heads // group_heads, group_heads * head_dim)
    norm_scale = lax.rsqrt(jnp.mean(grouped * grouped, axis=3, keepdims=True) + norm_eps)
    normed = (grouped * norm_scale).reshape(sessions, tokens, inner)
    normed = (normed * norm_gain).astype(jnp.bfloat16)
    partial_out = jnp.einsum(
        "stk,kd->std",
        normed,
        lax.all_gather(out_weight, "ctx", axis=1, tiled=True),
        preferred_element_type=jnp.float32,
    )
    summed = lax.psum_scatter(
        partial_out.astype(jnp.bfloat16), "head", scatter_dimension=2, tiled=True
    ).astype(jnp.float32)
    mixed = (summed * live_rows[:, :, None]).astype(jnp.bfloat16)
    end_state = jnp.exp(shard_log)[..., None, None] * carried + local_end
    whole_end = from_root(end_state.astype(jnp.bfloat16), "ctx", ctx_count - 1).astype(
        end_state.dtype
    )
    final_states = lax.dynamic_slice_in_dim(whole_end, ctx_index * state_cols, state_cols, 3)
    return (mixed, final_states)


def solution(mesh):
    placed = (
        P(("groups", "sess"), "ctx", "head"),
        P(("groups", "sess"), "ctx", "head"),
        P(("groups", "sess"), "ctx", None, None),
        P(("groups", "sess"), "ctx", None, None),
        P(("groups", "sess"), "ctx", "head"),
        P("head"),
        P("head"),
        P("head"),
        P("head"),
        P("head", "ctx"),
        P(("groups", "sess"), "head", None, "ctx"),
        P("groups"),
        P("groups"),
    )
    return jax.shard_map(
        shards,
        mesh=mesh,
        in_specs=placed,
        out_specs=(
            P(("groups", "sess"), "ctx", "head"),
            P(("groups", "sess"), "head", None, "ctx"),
        ),
        check_vma=False,
    )
```

profile of v0, /device:TPU:0, one launch (start us, length us, event | category | flops | bytes accessed | tf_op | source)
XLA Modules:
  0.0 939.3 jit_solution(13627045292249434513)
XLA Ops:
  7.2 0.0 all-gather.4.cloned.1.call-start
  7.2 4.0 convert_element_type.59
  11.2 0.0 all-gather.6.cloned.1.call-start
  11.3 0.1 compare_and_fusion
  11.4 16.4 %all-gather.4.cloned.1.call-done = bf16[8,64,64,32]{2,3,1,0:T(8,128)(2,1)} async-done(((bf16[4,64,64,32]{2,3,1,0:T(8,128)(2,1)}), bf16[8,64,64,32]{2,3,1,0:T(8,128)(2,1)}) %all-gather.4.cloned.1.call-update) | async-done | bytes 2097168 | tf_op jit(solution)/shard_map/all_gather | solution.py:55
  27.8 2.9 gather_fusion
  30.7 1.2 select_convert_fusion
  32.0 0.0 all-gather.8.cloned.1.call-start
  32.1 0.7 all-gather.8.cloned.1.call-update
  32.8 0.8 copy-done.1
  33.6 2.4 copy.86
  36.1 3.0 copy.92
  39.0 0.1 copy.81
  39.2 0.1 dynamic-slice_multiply_fusion
  39.2 0.1 compare_convert_fusion
  39.3 0.1 multiply_bitcast_fusion
  39.4 0.2 reduce_window_sum.19
  39.6 0.1 fusion.39
  39.7 0.1 copy.88
  39.8 0.1 copy.83
  39.9 0.1 copy.85
  40.1 0.1 copy.87
  40.1 0.1 copy.91
  40.3 0.3 constant_dynamic-slice_fusion
  40.7 0.3 fusion.35
  41.0 1.1 broadcast_in_dim.68
  42.0 17.8 %fusion.33 = f32[2,64,64,128]{3,2,1,0:T(8,128)} fusion(f32[2,128,64,128]{3,1,2,0:T(8,128)S(1)} %bitcast.69), kind=kOutput, calls=%fused_computation.41 | convolution fusion | flops 1610612736 | bytes 12582912 | tf_op jit(solution)/shard_map/sclhn,schpn->sclhp/dot_general | solution.py:106
  59.8 1.1 broadcast_in_dim.74
  60.9 0.5 copy-done.2
  61.4 9.1 fusion.27
  70.5 1.0 broadcast_in_dim.64
  71.6 11.9 %fusion.2 = f32[2,64,128,64]{2,3,1,0:T(8,128)} fusion(bf16[2,128,64,64]{1,3,2,0:T(8,128)(2,1)S(1)} %bitcast.76, f32[2,64,128,128]{3,2,1,0:T(8,128)S(1)} %bitcast.74, f32[2,64,128]{2,1,0:T(8,128)S(1)} %copy.85, f32[2,64,128]{2,1,0:T(8,128)S(1)} %copy.83, pred[128,128]{1,0:T(8,128)(4,1)S(1)} %iota_compare_fusion), kind=kOutput, calls=%fused_computation.5 | convolution fusion | flops 1621098496 | bytes 14827520 | tf_op jit(solution)/shard_map/schlm,scmhp->sclhp/dot_general | solution.py:92
  83.5 30.6 %all-gather.6.cloned.1.call-done = bf16[2,64,64,128]{2,3,1,0:T(8,128)(2,1)} async-done(((bf16[2,64,64,32]{2,3,1,0:T(8,128)(2,1)}), bf16[2,64,64,128]{2,3,1,0:T(8,128)(2,1)}) %all-gather.6.cloned.1.call-update) | async-done | bytes 2097168 | tf_op jit(solution)/shard_map/all_gather | solution.py:60
  114.1 5.2 copy.89
  119.3 6.7 copy.107
  125.9 393.2 %while.12 = (s32[]{:T(128)}, f32[2,64,64,128]{3,2,1,0:T(8,128)}, pred[]{:T(512)}, f32[2,64,1,1]{1,0,3,2:T(2,128)S(1)}, f32[2,64,64,128]{3,2,1,0:T(8,128)}, /*index=5*/f32[2,64,64,128]{3,2,1,0:T(8,128)}, s32[]{:T(128)}) while((s32[]{:T(128)}, f32[2,64,64,128]{3,2,1,0:T(8,128)}, pred[]{:T(512)}, f32[2,64,1,1]{1,0,3,2:T(2,128)S(1)}, ...), condition=%wide.region_2.3_spmd, body=%wide.region_1.2_spmd.sunk | while | flops 5242882 | bytes 29360756 | solution.py:115
  125.9 5.7 add_convert_fusion.3
  131.6 2.6 collective-permute-start
  134.2 89.2 %collective-permute-done = bf16[2,64,64,128]{3,2,1,0:T(8,128)(2,1)} collective-permute-done((bf16[2,64,64,128]{3,2,1,0:T(8,128)(2,1)S(1)}, bf16[2,64,64,128]{3,2,1,0:T(8,128)(2,1)}, u32[]{:S(2)}, u32[]{:S(2)}) %collective-permute-start) | collective-permute-done | bytes 2097184 | tf_op jit(solution)/shard_map/while/body/eval_jaxpr/ppermute | solution.py:16
  223.4 5.9 convert_select_fusion.2
  229.3 4.1 add_convert_fusion.3
  233.4 46.4 %collective-permute-start = (bf16[2,64,64,128]{3,2,1,0:T(8,128)(2,1)S(1)}, bf16[2,64,64,128]{3,2,1,0:T(8,128)(2,1)}, u32[]{:S(2)}, u32[]{:S(2)}) collective-permute-start(bf16[2,64,64,128]{3,2,1,0:T(8,128)(2,1)S(1)} %add_convert_fusion.3), channel_id=1, source_target_pairs={{0,4},{4,8},{8,12},{1,5},{5,9},{9,13},{2,6},{6,10},{10,14},{3,7},{... | collective-permute-start | bytes 6291464 | tf_op jit(solution)/shard_map/while/body/eval_jaxpr/ppermute | solution.py:16
  279.8 88.9 %collective-permute-done = bf16[2,64,64,128]{3,2,1,0:T(8,128)(2,1)} collective-permute-done((bf16[2,64,64,128]{3,2,1,0:T(8,128)(2,1)S(1)}, bf16[2,64,64,128]{3,2,1,0:T(8,128)(2,1)}, u32[]{:S(2)}, u32[]{:S(2)}) %collective-permute-start) | collective-permute-done | bytes 2097184 | tf_op jit(solution)/shard_map/while/body/eval_jaxpr/ppermute | solution.py:16
  368.7 5.9 convert_select_fusion.2
  374.7 4.0 add_convert_fusion.3
  378.7 49.8 %collective-permute-start = (bf16[2,64,64,128]{3,2,1,0:T(8,128)(2,1)S(1)}, bf16[2,64,64,128]{3,2,1,0:T(8,128)(2,1)}, u32[]{:S(2)}, u32[]{:S(2)}) collective-permute-start(bf16[2,64,64,128]{3,2,1,0:T(8,128)(2,1)S(1)} %add_convert_fusion.3), channel_id=1, source_target_pairs={{0,4},{4,8},{8,12},{1,5},{5,9},{9,13},{2,6},{6,10},{10,14},{3,7},{... | collective-permute-start | bytes 6291464 | tf_op jit(solution)/shard_map/while/body/eval_jaxpr/ppermute | solution.py:16
  428.4 84.8 %collective-permute-done = bf16[2,64,64,128]{3,2,1,0:T(8,128)(2,1)} collective-permute-done((bf16[2,64,64,128]{3,2,1,0:T(8,128)(2,1)S(1)}, bf16[2,64,64,128]{3,2,1,0:T(8,128)(2,1)}, u32[]{:S(2)}, u32[]{:S(2)}) %collective-permute-start) | collective-permute-done | bytes 2097184 | tf_op jit(solution)/shard_map/while/body/eval_jaxpr/ppermute | solution.py:16
  513.2 5.9 convert_select_fusion.2
  519.1 22.6 %fusion.17 = f32[2,1,128,64,64]{2,4,3,0,1:T(8,128)} fusion(f32[2,64,64,128]{3,2,1,0:T(8,128)} %fusion.33, f32[2,64,128,64]{2,3,1,0:T(8,128)} %fusion.2, f32[2,1,128,64,64]{2,4,3,0,1:T(8,128)} %bitcast.72, f32[2,64,64,128]{3,2,1,0:T(8,128)} %get-tuple-element.76, f32[2,128,64,128]{3,1,2,0:T(8,128)} %bitcast.70, f32[64]{0:T(128)S(1)} %copy-done.8, ...), kind=kOutput, calls=%fused_computation.21 | convolution fusion | flops 1616904192 | bytes 29491456 | tf_op jit(solution)/shard_map/sclhn,shpn->sclhp/dot_general | solution.py:118
  541.7 5.8 copy.93
  547.5 5.3 fusion.45
  552.9 6.0 mul.183
  558.9 2.8 reduce_sum.8
  561.7 2.6 mul.184
  564.3 6.1 mul.185
  570.4 5.5 fusion.30
  575.9 0.0 reduce-scatter.2.cloned.1.call-start
  576.0 230.1 %all-gather.8.cloned.1.call-done = bf16[4096,4096]{1,0:T(8,128)(2,1)} async-done(((bf16[4096,1024]{1,0:T(8,128)(2,1)}), bf16[4096,4096]{1,0:T(8,128)(2,1)}) %all-gather.8.cloned.1.call-update) | async-done | bytes 33554448 | tf_op jit(solution)/shard_map/all_gather | solution.py:130
  806.0 19.4 %fusion.9 = bf16[2,128,4096]{2,1,0:T(8,128)(2,1)} fusion(bf16[4096,4096]{1,0:T(8,128)(2,1)} %all-gather.8.cloned.1.call-done, f32[2,128,4096]{2,1,0:T(8,128)} %mul.185, f32[4096]{0:T(1024)S(1)} %copy-done.10, f32[2,128,4096]{2,1,0:T(8,128)} %copy.93, bf16[2,128,4096]{2,1,0:T(8,128)(2,1)S(1)} %copy-done.3), kind=kOutput, calls=%fused_computation.14 | convolution fusion | flops 8600420352 | bytes 46153728 | tf_op jit(solution)/shard_map/stk,kd->std/dot_general | solution.py:127
  825.5 71.8 %all-reduce.2.cloned.1.call-done = bf16[2,64,64,128]{3,2,1,0:T(8,128)(2,1)} async-done(((bf16[2,64,64,128]{3,2,1,0:T(8,128)(2,1)}), bf16[2,64,64,128]{3,2,1,0:T(8,128)(2,1)}) %all-reduce.2.cloned.1.call-update) | async-done | bytes 2097168 | tf_op jit(solution)/shard_map/psum | solution.py:21
  897.2 4.3 dynamic-slice_convert_fusion
  901.5 3.8 copy.96
  905.3 25.0 %reduce-scatter.2.cloned.1.call-done = bf16[2,128,2048]{2,1,0:T(8,128)(2,1)} async-done(((bf16[2,128,4096]{2,1,0:T(8,128)(2,1)}), bf16[2,128,2048]{2,1,0:T(8,128)(2,1)}) %reduce-scatter.2.cloned.1.call-update) | async-done | bytes 1048592 | tf_op jit(solution)/shard_map/reduce_scatter | solution.py:133
  930.3 2.4 multiply_convert_fusion.2
  (39 shorter events, 0.3 us)
Async XLA Ops:
  7.2 4.1 copy-start.9
  7.2 20.6 %all-gather.4.cloned.1.call-start = ((), (), s32[]{:S(2)}) async-start(), calls=%async_computation.1 | async-start | bytes 6291456 | tf_op jit(solution)/shard_map/all_gather | solution.py:55
  11.2 102.8 %all-gather.6.cloned.1.call-start = ((), (), s32[]{:S(2)}) async-start(), calls=%async_computation.2 | async-start | bytes 5242880 | tf_op jit(solution)/shard_map/all_gather | solution.py:60
  32.0 1.6 copy-start.1
  32.0 774.0 %all-gather.8.cloned.1.call-start = ((), (), s32[]{:S(2)}) async-start(), calls=%async_computation.3 | async-start | bytes 41943040 | tf_op jit(solution)/shard_map/all_gather | solution.py:130
  32.8 864.5 %all-reduce.2.cloned.1.call-start = ((), (), s32[]{:S(2)}) async-start(), calls=%async_computation.5 | async-start | bytes 4194304 | tf_op jit(solution)/shard_map/psum | solution.py:21
  36.0 3.0 copy-start.6
  36.0 3.1 copy-start.11
  36.0 3.2 copy-start.12
  36.0 3.3 copy-start.7
  36.0 4.2 copy-start.4
  36.1 4.2 copy-start.5
  42.0 17.8 %copy-start = (f32[2,128,4,16,128]{4,1,3,2,0:T(8,128)}, f32[2,128,4,16,128]{4,1,3,2,0:T(8,128)S(1)}, u32[]{:S(2)}) copy-start(f32[2,128,4,16,128]{4,1,3,2,0:T(8,128)S(1)} %broadcast_in_dim.68) | copy-start | bytes 25165828
  59.8 1.6 copy-start.2
  125.9 393.2 %copy-start.8 = (f32[64]{0:T(128)S(1)}, f32[64]{0:T(128)}, u32[]{:S(2)}) copy-start(f32[64]{0:T(128)} %param.22) | copy-start | bytes 772
  131.6 91.8 %collective-permute-start = (bf16[2,64,64,128]{3,2,1,0:T(8,128)(2,1)S(1)}, bf16[2,64,64,128]{3,2,1,0:T(8,128)(2,1)}, u32[]{:S(2)}, u32[]{:S(2)}) collective-permute-start(bf16[2,64,64,128]{3,2,1,0:T(8,128)(2,1)S(1)} %add_convert_fusion.3), channel_id=1, source_target_pairs={{0,4},{4,8},{8,12},{1,5},{5,9},{9,13},{2,6},{6,10},{10,14},{3,7},{... | collective-permute-start | bytes 6291464 | tf_op jit(solution)/shard_map/while/body/eval_jaxpr/ppermute | solution.py:16
  233.4 135.3 %collective-permute-start = (bf16[2,64,64,128]{3,2,1,0:T(8,128)(2,1)S(1)}, bf16[2,64,64,128]{3,2,1,0:T(8,128)(2,1)}, u32[]{:S(2)}, u32[]{:S(2)}) collective-permute-start(bf16[2,64,64,128]{3,2,1,0:T(8,128)(2,1)S(1)} %add_convert_fusion.3), channel_id=1, source_target_pairs={{0,4},{4,8},{8,12},{1,5},{5,9},{9,13},{2,6},{6,10},{10,14},{3,7},{... | collective-permute-start | bytes 6291464 | tf_op jit(solution)/shard_map/while/body/eval_jaxpr/ppermute | solution.py:16
  378.7 134.6 %collective-permute-start = (bf16[2,64,64,128]{3,2,1,0:T(8,128)(2,1)S(1)}, bf16[2,64,64,128]{3,2,1,0:T(8,128)(2,1)}, u32[]{:S(2)}, u32[]{:S(2)}) collective-permute-start(bf16[2,64,64,128]{3,2,1,0:T(8,128)(2,1)S(1)} %add_convert_fusion.3), channel_id=1, source_target_pairs={{0,4},{4,8},{8,12},{1,5},{5,9},{9,13},{2,6},{6,10},{10,14},{3,7},{... | collective-permute-start | bytes 6291464 | tf_op jit(solution)/shard_map/while/body/eval_jaxpr/ppermute | solution.py:16
  541.7 5.8 copy-start.3
  570.4 235.6 %copy-start.10 = (f32[4096]{0:T(1024)S(1)}, f32[4096]{0:T(1024)}, u32[]{:S(2)}) copy-start(f32[4096]{0:T(1024)} %param.23) | copy-start | bytes 49156
  575.9 354.4 %reduce-scatter.2.cloned.1.call-start = ((), (), s32[]{:S(2)}) async-start(), calls=%async_computation.4 | async-start | bytes 3145728 | tf_op jit(solution)/shard_map/reduce_scatter | solution.py:133
Sparse Core Ops, SparseCore 0:
  11.4 16.3 all-gather.3
  32.1 81.9 all-gather.5
  115.7 690.3 all-gather.7
  808.8 88.3 all-reduce.1
  899.3 30.9 reduce-scatter.1
where the time goes:
time: 940 us; the launch traced here: 939 us
  waiting for transfers between devices  637 us (68%)
  starting transfers between devices  99.1 us (11%)
  matrix products  81.1 us (9%)
  other arithmetic  57.8 us (6%)
  local copies, waits for them, and re-layouts  49.8 us (5%)
  between operations  14 us (1%)
    ppermute x3, waiting for transfers between devices, shifted(): return lax.ppermute(value, axis, pairs)  263 us
    all_gather x1, waiting for transfers between devices, shards(): lax.all_gather(out_weight, 'ctx', axis=1, tiled=True)  230 us
    ppermute x3, starting transfers between devices, shifted(): return lax.ppermute(value, axis, pairs)  98.8 us
    psum x1, waiting for transfers between devices, from_root(): return lax.psum(block, axis)  71.8 us
    all_gather x1, waiting for transfers between devices, shards(): lax.all_gather(start_cols.astype(jnp.bfloat16), 'ctx', axis=3, tiled=True)  30.6 us
    reduce_scatter x1, waiting for transfers between devices, shards(): lax.psum_scatter(partial_out.astype(jnp.bfloat16), 'head', scatter_dimens...  25 us
    dot_general x1, matrix products, shards(): jnp.einsum('sclhn,shpn->sclhp', c_heads, carried, precision=highest)  22.6 us
    dot_general x1, matrix products, shards(): jnp.einsum('stk,kd->std', normed, lax.all_gather(out_weight, 'ctx', axis=...  19.4 us
  transfers between devices with their start and end apart: 8, of which 8 were waited for; matrix products, arithmetic and copies ran while one was open for 19% of the time, Pallas kernels for 0%

commit v1 on v0

--- a/solution.py
+++ b/solution.py
@@ -1,3 +1,4 @@
+import functools
 import jax
 import jax.numpy as jnp
 from jax import lax
@@ -8,6 +9,15 @@
 SPAN = 128
 highest = lax.Precision.HIGHEST
 norm_eps = 1e-05
+
+
+def wrap_the_point(view, dim_no):
+    heard = jnp.stack([view for _ in range(lax.axis_size("ctx"))], axis=0)
+    w_next = lax.all_to_all(heard, "ctx", 0, 0)
+    return jnp.concatenate(w_next, dim_no)
+
+
+part_cards_on = functools.partial(wrap_the_point, dim_no=1)
 
 
 def shifted(value, axis, by):
@@ -125,10 +135,7 @@
     normed = (grouped * norm_scale).reshape(sessions, tokens, inner)
     normed = (normed * norm_gain).astype(jnp.bfloat16)
     partial_out = jnp.einsum(
-        "stk,kd->std",
-        normed,
-        lax.all_gather(out_weight, "ctx", axis=1, tiled=True),
-        preferred_element_type=jnp.float32,
+        "stk,kd->std", normed, part_cards_on(out_weight), preferred_element_type=jnp.float32
     )
     summed = lax.psum_scatter(
         partial_out.astype(jnp.bfloat16), "head", scatter_dimension=2, tiled=True

time: 940 us -> 1200 us (1.28)
  local copies, waits for them, and re-layouts: 49.8 us -> 157 us
  starting transfers between devices: 99.1 us -> 201 us
  waiting for transfers between devices: 637 us -> 686 us
    all_gather x1 -> x0, waiting for transfers between devices: 230 us -> none  [shards(): lax.all_gather(out_weight, 'ctx', axis=1, tiled=True)]
    all_gather x1, waiting for transfers between devices: 30.6 us -> 218 us  [shards(): lax.all_gather(start_cols.astype(jnp.bfloat16), 'ctx', axis=3, tiled=True)]
    ppermute x3, waiting for transfers between devices: 263 us -> 434 us  [shifted(): return lax.ppermute(value, axis, pairs)]
    reshape x0 -> x2, local copies, waits for them, and re-layouts: none -> 96.2 us  [wrap_the_point(): return jnp.concatenate(w_next, dim_no)]
    ppermute x3, starting transfers between devices: 98.8 us -> 191 us  [shifted(): return lax.ppermute(value, axis, pairs)]
    psum x1, waiting for transfers between devices: 71.8 us -> 0.02 us  [from_root(): return lax.psum(block, axis)]
    another operation x1 -> x2, local copies, waits for them, and re-layouts: 0.08 us -> 13.6 us  [the longest x1 13.5 us: wrap_the_point(): heard = jnp.stack([view for _ in range(lax.axis_size('ctx'))], axis=0)]
  transfers between devices with their start and end apart: 8 -> 8, of which waited for: 8 -> 6; matrix products, arithmetic and copies ran while one was open for 19% -> 23% of each run, Pallas kernels for 0% -> 0%
where the time goes in v1:
time: 1200 us
  waiting for transfers between devices  686 us (57%)
  starting transfers between devices  201 us (17%)
  local copies, waits for them, and re-layouts  157 us (13%)
  matrix products  81.5 us (7%)
  other arithmetic  56.4 us (5%)
  between operations  14.3 us (1%)
    ppermute x3, waiting for transfers between devices, shifted(): return lax.ppermute(value, axis, pairs)  434 us
    all_gather x1, waiting for transfers between devices, shards(): lax.all_gather(start_cols.astype(jnp.bfloat16), 'ctx', axis=3, tiled=True)  218 us
    ppermute x3, starting transfers between devices, shifted(): return lax.ppermute(value, axis, pairs)  191 us
    reshape x2, local copies, waits for them, and re-layouts, wrap_the_point(): return jnp.concatenate(w_next, dim_no)  96.2 us
    reduce_scatter x1, waiting for transfers between devices, shards(): lax.psum_scatter(partial_out.astype(jnp.bfloat16), 'head', scatter_dimens...  24.6 us
  transfers between devices with their start and end apart: 8, of which 6 were waited for; matrix products, arithmetic and copies ran while one was open for 23% of the time, Pallas kernels for 0%

profile of v1, /device:TPU:0, one launch (start us, length us, event | category | flops | bytes accessed | tf_op | source)
XLA Modules:
  0.0 1196.8 jit_solution(221705594596952937)
XLA Ops:
  7.2 13.5 %stack.2 = bf16[4,4096,1024]{2,1,0:T(8,128)(2,1)} broadcast(bf16[4096,1024]{1,0:T(8,128)(2,1)} %param.24), dimensions={1,2} | broadcast | bytes 41943040 | tf_op jit(solution)/shard_map/stack | solution.py:15
  20.6 9.7 all-to-all-start
  30.4 0.0 all-gather.3.cloned.1.call-start
  30.5 4.1 convert_element_type.59
  34.6 0.0 all-gather.5.cloned.1.call-start
  34.7 2.5 copy.88
  37.2 3.0 copy.94
  40.1 0.1 copy.83
  40.3 0.1 dynamic-slice_multiply_fusion
  40.4 0.1 compare_convert_fusion
  40.4 0.1 multiply_bitcast_fusion
  40.5 0.2 reduce_window_sum.19
  40.7 0.1 fusion.34
  40.9 0.1 copy.90
  40.9 0.1 copy.85
  41.1 0.1 copy.87
  41.1 0.1 compare_and_fusion
  41.3 10.1 all-gather.3.cloned.1.call-done
  51.3 2.9 gather_fusion
  54.2 1.2 select_convert_fusion
  55.5 0.0 all-reduce.2.cloned.1.call-start
  55.6 0.1 copy.89
  55.7 0.1 copy.93
  55.8 0.3 constant_dynamic-slice_fusion
  56.2 0.3 fusion.30
  56.5 1.1 broadcast_in_dim.68
  57.6 18.2 %fusion.28 = f32[2,64,64,128]{3,2,1,0:T(8,128)} fusion(f32[2,128,64,128]{3,1,2,0:T(8,128)S(1)} %bitcast.66), kind=kOutput, calls=%fused_computation.39 | convolution fusion | flops 1610612736 | bytes 12582912 | tf_op jit(solution)/shard_map/sclhn,schpn->sclhp/dot_general | solution.py:116
  75.8 1.1 broadcast_in_dim.74
  76.9 0.5 copy-done.2
  77.4 9.4 fusion.22
  86.8 1.1 broadcast_in_dim.64
  87.9 12.0 fusion
  99.8 217.8 %all-gather.5.cloned.1.call-done = bf16[2,64,64,128]{2,3,1,0:T(8,128)(2,1)} async-done(((bf16[2,64,64,32]{2,3,1,0:T(8,128)(2,1)}), bf16[2,64,64,128]{2,3,1,0:T(8,128)(2,1)}) %all-gather.5.cloned.1.call-update) | async-done | bytes 2097168 | tf_op jit(solution)/shard_map/all_gather | solution.py:70
  317.6 5.2 copy.91
  322.9 4.8 copy.110
  327.6 654.9 %while.12 = (s32[]{:T(128)}, f32[2,64,64,128]{3,2,1,0:T(8,128)}, pred[]{:T(512)}, f32[2,64,1,1]{1,0,3,2:T(2,128)S(1)}, f32[2,64,64,128]{3,2,1,0:T(8,128)}, /*index=5*/f32[2,64,64,128]{3,2,1,0:T(8,128)}, s32[]{:T(128)}) while((s32[]{:T(128)}, f32[2,64,64,128]{3,2,1,0:T(8,128)}, pred[]{:T(512)}, f32[2,64,1,1]{1,0,3,2:T(2,128)S(1)}, ...), condition=%wide.region_2.3_spmd, body=%wide.region_1.2_spmd.sunk | while | flops 5242882 | bytes 29360756 | solution.py:125
  327.8 4.0 add_convert_fusion.3
  331.8 2.6 collective-permute-start
  334.4 348.7 %collective-permute-done = bf16[2,64,64,128]{3,2,1,0:T(8,128)(2,1)} collective-permute-done((bf16[2,64,64,128]{3,2,1,0:T(8,128)(2,1)S(1)}, bf16[2,64,64,128]{3,2,1,0:T(8,128)(2,1)}, u32[]{:S(2)}, u32[]{:S(2)}) %collective-permute-start) | collective-permute-done | bytes 2097184 | tf_op jit(solution)/shard_map/while/body/eval_jaxpr/ppermute | solution.py:26
  683.2 5.9 convert_select_fusion.2
  689.1 4.0 add_convert_fusion.3
  693.1 184.0 %collective-permute-start = (bf16[2,64,64,128]{3,2,1,0:T(8,128)(2,1)S(1)}, bf16[2,64,64,128]{3,2,1,0:T(8,128)(2,1)}, u32[]{:S(2)}, u32[]{:S(2)}) collective-permute-start(bf16[2,64,64,128]{3,2,1,0:T(8,128)(2,1)S(1)} %add_convert_fusion.3), channel_id=1, source_target_pairs={{0,4},{4,8},{8,12},{1,5},{5,9},{9,13},{2,6},{6,10},{10,14},{3,7},{... | collective-permute-start | bytes 6291464 | tf_op jit(solution)/shard_map/while/body/eval_jaxpr/ppermute | solution.py:26
  877.1 43.0 %collective-permute-done = bf16[2,64,64,128]{3,2,1,0:T(8,128)(2,1)} collective-permute-done((bf16[2,64,64,128]{3,2,1,0:T(8,128)(2,1)S(1)}, bf16[2,64,64,128]{3,2,1,0:T(8,128)(2,1)}, u32[]{:S(2)}, u32[]{:S(2)}) %collective-permute-start) | collective-permute-done | bytes 2097184 | tf_op jit(solution)/shard_map/while/body/eval_jaxpr/ppermute | solution.py:26
  920.1 5.9 convert_select_fusion.2
  926.0 4.0 add_convert_fusion.3
  930.0 4.5 collective-permute-start
  934.5 42.1 %collective-permute-done = bf16[2,64,64,128]{3,2,1,0:T(8,128)(2,1)} collective-permute-done((bf16[2,64,64,128]{3,2,1,0:T(8,128)(2,1)S(1)}, bf16[2,64,64,128]{3,2,1,0:T(8,128)(2,1)}, u32[]{:S(2)}, u32[]{:S(2)}) %collective-permute-start) | collective-permute-done | bytes 2097184 | tf_op jit(solution)/shard_map/while/body/eval_jaxpr/ppermute | solution.py:26
  976.7 5.9 convert_select_fusion.2
  982.6 22.4 %fusion.12 = f32[2,1,128,64,64]{2,4,3,0,1:T(8,128)} fusion(f32[2,64,64,128]{3,2,1,0:T(8,128)} %fusion.28, f32[2,64,128,64]{2,3,1,0:T(8,128)} %fusion, f32[2,1,128,64,64]{2,4,3,0,1:T(8,128)} %bitcast.69, f32[2,64,64,128]{3,2,1,0:T(8,128)} %get-tuple-element.76, f32[2,128,64,128]{3,1,2,0:T(8,128)} %bitcast.67, f32[64]{0:T(128)S(1)} %copy-done.8, ...), kind=kOutput, calls=%fused_computation.19 | convolution fusion | flops 1616904192 | bytes 29491456 | tf_op jit(solution)/shard_map/sclhn,shpn->sclhp/dot_general | solution.py:128
  1004.9 5.6 copy.95
  1010.6 5.6 fusion.25
  1016.2 0.0 reduce-scatter.2.cloned.1.call-start
  1016.2 5.3 fusion.40
  1021.6 6.5 mul.183
  1028.0 2.8 reduce_sum.8
  1030.9 2.6 mul.184
  1033.5 6.0 mul.185
  1039.5 42.1 %copy.98 = bf16[4096,4,1024]{2,1,0:T(4,128)(2,1)} copy(bf16[4096,4,1024]{2,0,1:T(8,128)(2,1)} %bitcast.28) | data formatting | bytes 67108864 | tf_op jit(solution)/shard_map/reshape | solution.py:17
  1081.6 54.1 %reshape.230 = bf16[4096,4096,1]{1,0,2:T(8,128)(2,1)} reshape(bf16[4096,4,1024]{2,1,0:T(4,128)(2,1)} %copy.98) | data formatting | bytes 67108864 | tf_op jit(solution)/shard_map/reshape | solution.py:17
  1135.7 19.2 %convolution_convert_fusion = bf16[2,128,4096]{2,1,0:T(8,128)(2,1)} fusion(bf16[4096,4096,1]{1,0,2:T(8,128)(2,1)} %reshape.230, f32[2,128,4096]{2,1,0:T(8,128)} %mul.185, f32[4096]{0:T(1024)S(1)} %copy-done.10, f32[2,128,4096]{2,1,0:T(8,128)} %copy.95, bf16[2,128,4096]{2,1,0:T(8,128)(2,1)S(1)} %copy-done.3), kind=kOutput, calls=%fused_computation.12 | convolution fusion | flops 8600420352 | bytes 46153728 | tf_op jit(solution)/shard_map/stk,kd->std/dot_general | solution.py:137
  1155.0 4.3 dynamic-slice_convert_fusion
  1159.3 3.8 copy.99
  1163.1 24.6 %reduce-scatter.2.cloned.1.call-done = bf16[2,128,2048]{2,1,0:T(8,128)(2,1)} async-done(((bf16[2,128,4096]{2,1,0:T(8,128)(2,1)}), bf16[2,128,2048]{2,1,0:T(8,128)(2,1)}) %reduce-scatter.2.cloned.1.call-update) | async-done | bytes 1048592 | tf_op jit(solution)/shard_map/reduce_scatter | solution.py:140
  1187.6 2.4 multiply_convert_fusion.2
  (41 shorter events, 0.3 us)
Async XLA Ops:
  20.6 1018.9 %all-to-all-start = ((bf16[4,4096,1024]{2,1,0:T(8,128)(2,1)}), bf16[4,4096,1024]{2,1,0:T(8,128)(2,1)}, u32[]{:S(2)}, u32[]{:S(2)}) async-start(bf16[4,4096,1024]{2,1,0:T(8,128)(2,1)} %stack.2), calls=%async_computation | async-start | bytes 67108864 | tf_op jit(solution)/shard_map/all_to_all | solution.py:16
  30.4 4.3 copy-start.1
  30.4 20.9 %all-gather.3.cloned.1.call-start = ((), (), s32[]{:S(2)}) async-start(), calls=%async_computation.2 | async-start | bytes 6291456 | tf_op jit(solution)/shard_map/all_gather | solution.py:65
  34.6 283.0 %all-gather.5.cloned.1.call-start = ((), (), s32[]{:S(2)}) async-start(), calls=%async_computation.3 | async-start | bytes 5242880 | tf_op jit(solution)/shard_map/all_gather | solution.py:70
  37.2 3.0 copy-start.6
  37.2 3.1 copy-start.11
  37.2 3.2 copy-start.12
  37.2 3.3 copy-start.7
  37.2 4.0 copy-start.9
  41.0 14.8 %copy-start.4 = (bf16[2,128,8,128]{3,2,1,0:T(8,128)(2,1)S(1)}, bf16[2,128,8,128]{3,2,1,0:T(8,128)(2,1)}, u32[]{:S(2)}) copy-start(bf16[2,128,8,128]{3,2,1,0:T(8,128)(2,1)} %param.17) | copy-start | bytes 1572868
  41.0 14.8 %copy-start.5 = (bf16[2,128,8,128]{3,2,1,0:T(8,128)(2,1)S(1)}, bf16[2,128,8,128]{3,2,1,0:T(8,128)(2,1)}, u32[]{:S(2)}) copy-start(bf16[2,128,8,128]{3,2,1,0:T(8,128)(2,1)} %param.18) | copy-start | bytes 1572868
  55.5 1099.5 %all-reduce.2.cloned.1.call-start = ((), (), s32[]{:S(2)}) async-start(), calls=%async_computation.5 | async-start | bytes 4194304 | tf_op jit(solution)/shard_map/psum | solution.py:31
  57.6 18.2 %copy-start = (f32[2,128,4,16,128]{4,1,3,2,0:T(8,128)}, f32[2,128,4,16,128]{4,1,3,2,0:T(8,128)S(1)}, u32[]{:S(2)}) copy-start(f32[2,128,4,16,128]{4,1,3,2,0:T(8,128)S(1)} %broadcast_in_dim.68) | copy-start | bytes 25165828
  75.8 1.6 copy-start.2
  327.6 654.9 %copy-start.8 = (f32[64]{0:T(128)S(1)}, f32[64]{0:T(128)}, u32[]{:S(2)}) copy-start(f32[64]{0:T(128)} %param.22) | copy-start | bytes 772
  331.8 351.4 %collective-permute-start = (bf16[2,64,64,128]{3,2,1,0:T(8,128)(2,1)S(1)}, bf16[2,64,64,128]{3,2,1,0:T(8,128)(2,1)}, u32[]{:S(2)}, u32[]{:S(2)}) collective-permute-start(bf16[2,64,64,128]{3,2,1,0:T(8,128)(2,1)S(1)} %add_convert_fusion.3), channel_id=1, source_target_pairs={{0,4},{4,8},{8,12},{1,5},{5,9},{9,13},{2,6},{6,10},{10,14},{3,7},{... | collective-permute-start | bytes 6291464 | tf_op jit(solution)/shard_map/while/body/eval_jaxpr/ppermute | solution.py:26
  693.1 227.0 %collective-permute-start = (bf16[2,64,64,128]{3,2,1,0:T(8,128)(2,1)S(1)}, bf16[2,64,64,128]{3,2,1,0:T(8,128)(2,1)}, u32[]{:S(2)}, u32[]{:S(2)}) collective-permute-start(bf16[2,64,64,128]{3,2,1,0:T(8,128)(2,1)S(1)} %add_convert_fusion.3), channel_id=1, source_target_pairs={{0,4},{4,8},{8,12},{1,5},{5,9},{9,13},{2,6},{6,10},{10,14},{3,7},{... | collective-permute-start | bytes 6291464 | tf_op jit(solution)/shard_map/while/body/eval_jaxpr/ppermute | solution.py:26
  930.0 46.7 %collective-permute-start = (bf16[2,64,64,128]{3,2,1,0:T(8,128)(2,1)S(1)}, bf16[2,64,64,128]{3,2,1,0:T(8,128)(2,1)}, u32[]{:S(2)}, u32[]{:S(2)}) collective-permute-start(bf16[2,64,64,128]{3,2,1,0:T(8,128)(2,1)S(1)} %add_convert_fusion.3), channel_id=1, source_target_pairs={{0,4},{4,8},{8,12},{1,5},{5,9},{9,13},{2,6},{6,10},{10,14},{3,7},{... | collective-permute-start | bytes 6291464 | tf_op jit(solution)/shard_map/while/body/eval_jaxpr/ppermute | solution.py:26
  1010.6 5.7 copy-start.3
  1016.2 171.5 %reduce-scatter.2.cloned.1.call-start = ((), (), s32[]{:S(2)}) async-start(), calls=%async_computation.4 | async-start | bytes 3145728 | tf_op jit(solution)/shard_map/reduce_scatter | solution.py:140
  1081.6 54.1 %copy-start.10 = (f32[4096]{0:T(1024)S(1)}, f32[4096]{0:T(1024)}, u32[]{:S(2)}) copy-start(f32[4096]{0:T(1024)} %param.23) | copy-start | bytes 49156
Sparse Core Ops, SparseCore 0:
  34.8 16.5 all-gather.2
  55.6 261.9 all-gather.4
  1016.3 86.7 all-reduce.1
  1155.1 32.4 reduce-scatter.1
